TPU v7x, 128 devices: a whole 4x4x4 slice. The times are simulated.
128 devices in a mesh: front: 4 (over z_lo, core), grid: 32 (over z_hi, y, x).
Axes of the slice: x: 4, y: 4, z: 4 (z_hi: 2, z_lo: 2; z = z_hi * 2 + z_lo), core: 2. Of those that a mesh axis runs over, the one named last changes fastest.
Arguments:
- index_map: int32 [4, 8192], P('front'), may hold values from 0 to 16383, as said below
- lengths: int32 [4], P('front'), may hold values from 1 to 8192, 24576 in all
- update_front: float32 [4, 8192, 8192], P('front', 'grid'), may hold values from -0.0625 to 0.0625
- front_matrix: float32 [16384, 16384], P(('front', 'grid')), may hold values from -0.046875 to 0.046875
- random: float32 [16384, 256], P(('front', 'grid')), may hold values from -6 to 6
Outputs:
- parent_sample: float32 [16384, 256], P(('front', 'grid'))
Inputs may be any that keep to these rules, and one draw needn't show every extreme that they name: `index_map`: within one child the 8192 entries are distinct parent rows. `lengths`: rows of a child at or past its length are not live; the largest length equals 8192.
All inputs are finite; a program needn't handle non-finite values. No bound on the sum of `lengths` on one device may be relied on, other than what follows from the above.
Results may differ from a plain program's by a relative error of at most 0.0003.
Values sent between devices are 32-bit elements; how exact they have to be, the bound alone decides.
No kernel may reach another device: no remote copies, remote signals or barrier semaphores. Data moves between devices by JAX's collectives and lax.ppermute only.
A program may use at most 128 MiB of HBM per device.

v0:
```python
import jax
import jax.numpy as jnp
from jax import lax
from jax.sharding import PartitionSpec as P


def split_up(array, dim, length):
    shape = array.shape
    blocks = array.reshape(*shape[:dim], length, shape[dim] // length, *shape[dim + 1 :])
    return jnp.moveaxis(blocks, dim, 0)


def sum_at_owner(array, axis, dim):
    length = lax.axis_size(axis)
    blocks = lax.all_to_all(split_up(array, dim, length), axis, 0, 0, tiled=True)
    return jnp.sum(blocks, axis=0)


def shards(index_map, lengths, update_front, front_matrix, random):
    gathered_random = lax.all_gather(random, ("front", "grid"), axis=0, tiled=True)
    parent_part = jnp.dot(
        front_matrix,
        gathered_random,
        preferred_element_type=jnp.float32,
        precision=lax.Precision.HIGHEST,
    )
    index_rows = index_map[0]
    child_random = jnp.take(gathered_random, index_rows, axis=0)
    child_sample = jnp.dot(
        update_front[0],
        child_random,
        preferred_element_type=jnp.float32,
        precision=lax.Precision.HIGHEST,
    )
    local_rows = child_sample.shape[0]
    first_row = lax.axis_index("grid") * local_rows
    row_numbers = first_row + jnp.arange(local_rows, dtype=jnp.int32)
    live_rows = row_numbers < lengths[0]
    child_sample = jnp.where(live_rows[:, None], child_sample, jnp.float32(0.0))
    own_rows = parent_part.shape[0]
    group_sample = lax.all_gather(child_sample, "grid", axis=0, tiled=True)
    group_count = lax.axis_size("front")
    grid_count = lax.axis_size("grid")
    grid_place = lax.axis_index("grid")
    block_ids = jnp.arange(group_count, dtype=jnp.int32)[:, None] * grid_count + grid_place
    targets = (block_ids * own_rows + jnp.arange(own_rows, dtype=jnp.int32)[None, :]).reshape(-1)
    one_hot = (targets[:, None] == index_rows[None, :]).astype(jnp.float32)
    terms = jnp.dot(
        one_hot, group_sample, preferred_element_type=jnp.float32, precision=lax.Precision.HIGHEST
    )
    terms = terms.reshape(group_count, own_rows, terms.shape[1])
    added = sum_at_owner(terms, "front", 0)[0]
    return parent_part + added


def solution(mesh):
    placed = (
        P("front", None),
        P("front"),
        P("front", "grid", None),
        P(("front", "grid"), None),
        P(("front", "grid"), None),
    )
    return jax.shard_map(
        shards, mesh=mesh, in_specs=placed, out_specs=P(("front", "grid"), None), check_vma=False
    )
```

profile of v0, /device:TPU:1, one launch (start us, length us, event | category | flops | bytes accessed | tf_op | source)
XLA Modules:
  0.0 560.7 jit_solution(7659049847696991834)
XLA Ops:
  6.5 0.0 all-gather.3.cloned.1.call-start
  6.5 0.7 all-gather.3.cloned.1.call-update
  7.3 0.0 all-gather.5.cloned.1.call-start
  8.0 0.8 compare_and_fusion
  8.7 0.8 compare_select_fusion
  9.6 329.9 %all-gather.3.cloned.1.call-done = f32[16384,256]{1,0:T(8,128)} async-done(((f32[128,256]{1,0:T(8,128)}), f32[16384,256]{1,0:T(8,128)}) %all-gather.3.cloned.1.call-update) | async-done | bytes 16777232 | tf_op jit(solution)/shard_map/all_gather | solution.py:20
  339.5 37.3 %gather_fusion = f32[8192,256]{1,0:T(8,128)} fusion(f32[16384,256]{1,0:T(8,128)} %all-gather.3.cloned.1.call-done, s32[8192]{0:T(1024)S(1)} %broadcast_clamp_fusion), kind=kCustom, calls=%fused_computation | custom fusion | bytes 16809984 | tf_op jit(solution)/shard_map/jit(_take)/gather | solution.py:28
  376.8 0.0 copy-start
  376.8 21.5 %fusion.14 = f32[256,256]{0,1:T(8,128)} fusion(f32[1,256,8192]{2,1,0:T(8,128)} %param.7, f32[8192,256]{1,0:T(8,128)} %gather_fusion, pred[8192]{0:T(1024)(128)(4,1)S(1)} %compare_and_fusion, pred[256]{0:T(512)(128)(4,1)S(1)} %add_compare_fusion), kind=kOutput, calls=%fused_computation.11 | convolution fusion | flops 6444613632 | bytes 17047808 | tf_op jit(solution)/shard_map/dot_general | solution.py:29
  398.3 0.0 all-gather.5.cloned.1.call-update
  398.3 0.1 add_bitcast_fusion
  398.4 119.7 %all-gather.5.cloned.1.call-done = f32[8192,256]{0,1:T(8,128)} async-done(((f32[256,256]{0,1:T(8,128)}), f32[8192,256]{0,1:T(8,128)}) %all-gather.5.cloned.1.call-update) | async-done | bytes 8388624 | tf_op jit(solution)/shard_map/all_gather | solution.py:41
  518.1 0.0 copy-done
  518.1 10.6 %fusion = f32[512,256]{1,0:T(8,128)S(1)} fusion(f32[8192,256]{0,1:T(8,128)} %all-gather.5.cloned.1.call-done, s32[8192]{0:T(1024)S(1)} %bitcast.25, s32[512]{0:T(512)S(1)} %add_bitcast_fusion), kind=kOutput, calls=%fused_computation.1 | convolution fusion | flops 12889096192 | bytes 8947712 | tf_op jit(solution)/shard_map/dot_general | solution.py:48
  528.7 11.7 %all_to_all.5 = f32[4,1,128,256]{3,2,1,0:T(8,128)S(1)} all-to-all(f32[4,1,128,256]{3,2,1,0:T(8,128)S(1)} %bitcast.23), channel_id=1, replica_groups=mesh['front'=4,'grid'=32] {'front'}, dimensions={0} | all-to-all | bytes 1048576 | tf_op jit(solution)/shard_map/all_to_all | solution.py:15
  540.4 13.4 %convolution_add_fusion = f32[128,256]{1,0:T(8,128)} fusion(f32[128,256]{1,0:T(8,128)S(1)} %reduce_sum.9, f32[128,16384]{1,0:T(8,128)} %param.8, f32[16384,256]{1,0:T(8,128)} %all-gather.3.cloned.1.call-done), kind=kOutput, calls=%fused_computation.12 | convolution fusion | flops 6442483712 | bytes 25427968 | tf_op jit(solution)/shard_map/dot_general | solution.py:21
  (4 shorter events, 0.1 us)
Async XLA Ops:
  6.5 333.0 %all-gather.3.cloned.1.call-start = ((), (), s32[]{:S(2)}) async-start(), calls=%async_computation.1 | async-start | bytes 16908288 | tf_op jit(solution)/shard_map/all_gather | solution.py:20
  7.3 510.8 %all-gather.5.cloned.1.call-start = ((), (), s32[]{:S(2)}) async-start(), calls=%async_computation.2 | async-start | bytes 8650752 | tf_op jit(solution)/shard_map/all_gather | solution.py:41
  376.8 141.3 %copy-start = (s32[1,8192]{1,0:T(1,128)S(1)}, s32[1,8192]{1,0:T(1,128)}, u32[]{:S(2)}) copy-start(s32[1,8192]{1,0:T(1,128)} %param.5) | copy-start | bytes 98308
Sparse Core Ops, SparseCore 0:
  9.0 330.3 all-gather.2
  398.4 119.6 all-gather.4
where the time goes:
time: 561 us
  waiting for transfers between devices  450 us (80%)
  matrix products  45.5 us (8%)
  local copies, waits for them, and re-layouts  37.3 us (7%)
  between operations  14.1 us (3%)
  blocking collectives  11.7 us (2%)
    all_gather x1, waiting for transfers between devices, shards(): lax.all_gather(random, ('front', 'grid'), axis=0, tiled=True)  330 us
    all_gather x1, waiting for transfers between devices, shards(): group_sample = lax.all_gather(child_sample, 'grid', axis=0, tiled=True)  120 us
    gather x1, local copies, waits for them, and re-layouts, shards(): child_random = jnp.take(gathered_random, index_rows, axis=0)  37.3 us
    dot_general x1, matrix products, shards(): jnp.dot(update_front[0], child_random, preferred_element_type=jnp.float32...  21.5 us
    dot_general x1, matrix products, shards(): jnp.dot(front_matrix, gathered_random, preferred_element_type=jnp.float32...  13.4 us
    all_to_all x1, blocking collectives, sum_at_owner(): lax.all_to_all(split_up(array, dim, length), axis, 0, 0, tiled=True)  11.7 us
  transfers between devices with their start and end apart: 2, of which 2 were waited for; matrix products, arithmetic and copies ran while one was open for 0% of the time, Pallas kernels for 0%

commit v1 on v0

--- a/solution.py
+++ b/solution.py
@@ -38,7 +38,10 @@
     live_rows = row_numbers < lengths[0]
     child_sample = jnp.where(live_rows[:, None], child_sample, jnp.float32(0.0))
     own_rows = parent_part.shape[0]
-    group_sample = lax.all_gather(child_sample, "grid", axis=0, tiled=True)
+    size = lax.axis_size("grid")
+    parts = jnp.stack([child_sample for _ in range(size)])
+    parts = lax.all_to_all(parts, "grid", split_axis=0, concat_axis=0)
+    group_sample = jnp.concatenate(parts, axis=0)
     group_count = lax.axis_size("front")
     grid_count = lax.axis_size("grid")
     grid_place = lax.axis_index("grid")

time: 561 us -> 590 us (1.052); the launches traced: 561 us -> 581 us
  starting transfers between devices: 0.04 us -> 9.16 us
  waiting for transfers between devices: 450 us -> 459 us
    all_to_all x0 -> x1, waiting for transfers between devices: none -> 129 us  [shards(): parts = lax.all_to_all(parts, 'grid', split_axis=0, concat_axis=0)]
    all_gather x1 -> x0, waiting for transfers between devices: 120 us -> none  [shards(): group_sample = lax.all_gather(child_sample, 'grid', axis=0, tiled=True)]
    all_to_all x0 -> x1, starting transfers between devices: none -> 9.16 us  [shards(): parts = lax.all_to_all(parts, 'grid', split_axis=0, concat_axis=0)]
where the time goes in v1:
time: 590 us; the launch traced here: 581 us
  waiting for transfers between devices  459 us (78%)
  matrix products  44.7 us (8%)
  local copies, waits for them, and re-layouts  41.5 us (7%)
  between operations  14.1 us (2%)
  blocking collectives  10.7 us (2%)
  starting transfers between devices  9.16 us (2%)
    all_gather x1, waiting for transfers between devices, shards(): lax.all_gather(random, ('front', 'grid'), axis=0, tiled=True)  330 us
    all_to_all x1, waiting for transfers between devices, shards(): parts = lax.all_to_all(parts, 'grid', split_axis=0, concat_axis=0)  129 us
    gather x1, local copies, waits for them, and re-layouts, shards(): child_random = jnp.take(gathered_random, index_rows, axis=0)  37.2 us
    dot_general x1, matrix products, shards(): jnp.dot(update_front[0], child_random, preferred_element_type=jnp.float32...  20.8 us
    dot_general x1, matrix products, shards(): jnp.dot(front_matrix, gathered_random, preferred_element_type=jnp.float32...  13.4 us
  transfers between devices with their start and end apart: 2, of which 2 were waited for; matrix products, arithmetic and copies ran while one was open for 0% of the time, Pallas kernels for 0%

profile of v1, /device:TPU:1, one launch (start us, length us, event | category | flops | bytes accessed | tf_op | source)
XLA Modules:
  0.0 581.1 jit_solution(851023029194631223)
XLA Ops:
  6.5 0.0 all-gather.2.cloned.1.call-start
  6.5 0.7 all-gather.2.cloned.1.call-update
  7.9 0.8 compare_and_fusion
  8.7 0.8 compare_select_fusion
  9.5 330.0 %all-gather.2.cloned.1.call-done = f32[16384,256]{1,0:T(8,128)} async-done(((f32[128,256]{1,0:T(8,128)}), f32[16384,256]{1,0:T(8,128)}) %all-gather.2.cloned.1.call-update) | async-done | bytes 16777232 | tf_op jit(solution)/shard_map/all_gather | solution.py:20
  339.5 37.2 %gather_fusion = f32[8192,256]{1,0:T(8,128)} fusion(f32[16384,256]{1,0:T(8,128)} %all-gather.2.cloned.1.call-done, s32[8192]{0:T(1024)S(1)} %broadcast_clamp_fusion), kind=kCustom, calls=%fused_computation | custom fusion | bytes 16809984 | tf_op jit(solution)/shard_map/jit(_take)/gather | solution.py:28
  376.7 20.8 %fusion.17 = f32[256,256]{0,1:T(8,128)S(1)} fusion(f32[1,256,8192]{2,1,0:T(8,128)} %param.7, f32[8192,256]{1,0:T(8,128)} %gather_fusion, pred[8192]{0:T(1024)(128)(4,1)S(1)} %compare_and_fusion, pred[256]{0:T(512)(128)(4,1)S(1)} %add_compare_fusion), kind=kOutput, calls=%fused_computation.12 | convolution fusion | flops 6444613632 | bytes 17047808 | tf_op jit(solution)/shard_map/dot_general | solution.py:29
  397.4 0.1 copy.8
  397.6 4.2 stack.2
  401.7 0.0 copy-start
  401.7 9.2 %all-to-all-start = ((f32[32,256,256]{2,1,0:T(8,128)}), f32[32,256,256]{2,1,0:T(8,128)}, u32[]{:S(2)}, u32[]{:S(2)}) async-start(f32[32,256,256]{2,1,0:T(8,128)} %stack.2), calls=%async_computation | async-start | bytes 16777216 | tf_op jit(solution)/shard_map/all_to_all | solution.py:43
  410.9 0.1 iota_add_fusion
  411.0 128.5 %all-to-all-done = f32[32,256,256]{2,1,0:T(8,128)} async-done(((f32[32,256,256]{2,1,0:T(8,128)}), f32[32,256,256]{2,1,0:T(8,128)}, u32[]{:S(2)}, u32[]{:S(2)}) %all-to-all-start) | async-done | bytes 8388640 | tf_op jit(solution)/shard_map/all_to_all | solution.py:43
  539.5 0.0 copy-done
  539.5 10.5 %fusion.9 = f32[4,1,128,256]{3,2,1,0:T(8,128)S(1)} fusion(f32[8192,256,1]{1,0,2:T(8,128)} %bitcast.7, s32[8192]{0:T(1024)S(1)} %bitcast.26, s32[4,128]{1,0:T(4,128)S(1)} %iota_add_fusion), kind=kOutput, calls=%fused_computation.10 | convolution fusion | flops 12889096192 | bytes 8947712 | tf_op jit(solution)/shard_map/dot_general | solution.py:51
  550.1 10.7 %all_to_all.10 = f32[4,1,128,256]{3,2,1,0:T(8,128)S(1)} all-to-all(f32[4,1,128,256]{3,2,1,0:T(8,128)S(1)} %fusion.9), channel_id=1, replica_groups=mesh['front'=4,'grid'=32] {'front'}, dimensions={0} | all-to-all | bytes 1048576 | tf_op jit(solution)/shard_map/all_to_all | solution.py:15
  560.8 13.4 %convolution_add_fusion = f32[128,256]{1,0:T(8,128)} fusion(f32[128,256]{1,0:T(8,128)S(1)} %reduce_sum.9, f32[128,16384]{1,0:T(8,128)} %param.8, f32[16384,256]{1,0:T(8,128)} %all-gather.2.cloned.1.call-done), kind=kOutput, calls=%fused_computation.13 | convolution fusion | flops 6442483712 | bytes 25427968 | tf_op jit(solution)/shard_map/dot_general | solution.py:21
  (4 shorter events, 0.1 us)
Async XLA Ops:
  6.5 333.0 %all-gather.2.cloned.1.call-start = ((), (), s32[]{:S(2)}) async-start(), calls=%async_computation.2 | async-start | bytes 16908288 | tf_op jit(solution)/shard_map/all_gather | solution.py:20
  401.7 137.8 %copy-start = (s32[1,8192]{1,0:T(1,128)S(1)}, s32[1,8192]{1,0:T(1,128)}, u32[]{:S(2)}) copy-start(s32[1,8192]{1,0:T(1,128)} %param.5) | copy-start | bytes 98308
  401.7 137.8 %all-to-all-start = ((f32[32,256,256]{2,1,0:T(8,128)}), f32[32,256,256]{2,1,0:T(8,128)}, u32[]{:S(2)}, u32[]{:S(2)}) async-start(f32[32,256,256]{2,1,0:T(8,128)} %stack.2), calls=%async_computation | async-start | bytes 16777216 | tf_op jit(solution)/shard_map/all_to_all | solution.py:43
Sparse Core Ops, SparseCore 0:
  9.0 330.3 all-gather.1
